TPU v7x, 32 devices: a whole 2x2x4 slice. The times are simulated.
32 devices in a mesh: feeder: 8 (over z, core), tm: 4 (over y, x).
Axes of the slice: x: 2, y: 2, z: 4, core: 2. Of those that a mesh axis runs over, the one named last changes fastest.
Arguments:
- node_load: bfloat16 [128, 64, 24, 512], P('feeder', None, 'tm'), may hold values from -6 to 6
- drive_map: bfloat16 [128, 512, 256], P('feeder'), may hold values from -0.25 to 0.25
- decay_rate: float32 [128, 24, 256], P('feeder', 'tm'), may hold values from 0.45 to 1
- counts: int32 [128], P('feeder'), may hold values from 64 to 256
- out_map: float32 [128, 2, 256], P('feeder'), may hold values from -0.375 to 0.375
- area_of: int32 [128, 1], replicated, may hold values from 0 to 7; in each aligned block of 16 rows (0 to 15, 16 to 31, ...) at most 2 rows name the same one
- head_bus: int32 [128], replicated, may hold values from 0 to 255
- rule_of: int32 [128], replicated, may hold values from 0 to 15
- rule_knots: int32 [16, 8], replicated, may hold values from -3200 to 2400, as said below
- levels: int32 [16, 8], replicated, may hold values from -1000 to 1000
- sensitivity: float32 [8, 2, 256, 256], P('feeder'), may hold values from -0.6 to 0.6
Outputs:
- setpoints: float32 [128, 24, 64], P('feeder', 'tm')
Inputs may be any that keep to these rules, and one draw needn't show every extreme that they name: `area_of`: in each aligned block of 16 feeders no area is named by more than 2 feeders, a bound that some block reaches. `rule_knots`: each row strictly increasing, neighbouring breakpoints 200 to 800 apart.
All inputs are finite; a program needn't handle non-finite values.
Results may differ from a plain program's by a relative error of at most 0.00045.
Values sent between devices are 32-bit elements; how exact they have to be, the bound alone decides.
A program may use at most 64 MiB of HBM per device.

v0:
```python
import jax
import jax.numpy as jnp
from jax import lax
from jax.sharding import PartitionSpec as P

CAP = 2


def passed_along(block, axis, distance):
    devices = range(lax.axis_size(axis))
    route = [(i - distance, i) for i in devices if i - distance in devices]
    return lax.ppermute(block, axis, route)


def setpoint_rule(volts, knot_volts, knot_levels):
    result = knot_levels[..., 0:1] + jnp.zeros_like(volts)
    for piece in range(knot_volts.shape[-1] - 1):
        span_width = knot_volts[..., piece + 1 : piece + 2] - knot_volts[..., piece : piece + 1]
        slope = (
            knot_levels[..., piece + 1 : piece + 2] - knot_levels[..., piece : piece + 1]
        ) / span_width
        result = result + slope * jnp.clip(
            volts - knot_volts[..., piece : piece + 1], 0.0, span_width
        )
    return result


def per_device(
    node_load,
    drive_map,
    decay_rate,
    counts,
    out_map,
    area_of,
    head_bus,
    rule_of,
    rule_knots,
    levels,
    sensitivity,
):
    per_dev, scenarios, span_len, node_count = node_load.shape
    state_width = drive_map.shape[2]
    bus_count = sensitivity.shape[2]
    state_ids = jnp.arange(state_width, dtype=jnp.int32)
    live = (state_ids[None, :] < counts[:, None]).astype(jnp.float32)
    drive = (
        jnp.einsum("fctn,fns->fcts", node_load, drive_map, preferred_element_type=jnp.float32)
        * live[:, None, None, :]
    )
    local_state = jnp.zeros((per_dev, scenarios, state_width), jnp.float32)
    decay_prod = jnp.ones((per_dev, state_width), jnp.float32)
    history_record = []
    products = []
    for moment in range(span_len):
        retain = decay_rate[:, moment, :]
        local_state = retain[:, None, :] * local_state + drive[:, :, moment, :]
        decay_prod = decay_prod * retain
        history_record.append(local_state)
        products.append(decay_prod)

    def one_turn(turn_index, incoming):
        return passed_along(local_state + decay_prod[:, None, :] * incoming, "tm", 1)

    incoming = lax.fori_loop(0, lax.axis_size("tm") - 1, one_turn, jnp.zeros_like(local_state))
    states = (
        jnp.stack(history_record, 2)
        + jnp.stack(products, 1)[:, None, :, :] * incoming[:, :, None, :]
    )
    head_flow = jnp.einsum("fcts,fks->fktc", states, out_map, precision=lax.Precision.HIGHEST)
    head_flow = head_flow.reshape(per_dev, 2, span_len * scenarios)
    area_ids = area_of[:, 0]
    owner = lax.axis_index("feeder")
    rule_count = rule_knots.shape[0]
    rule_hot = (rule_of[:, None] == jnp.arange(rule_count, dtype=jnp.int32)[None, :]).astype(
        jnp.float32
    )
    knot_volts = (
        jnp.dot(rule_hot, rule_knots.astype(jnp.float32), precision=lax.Precision.HIGHEST) / 1000.0
    )
    knot_levels = (
        jnp.dot(rule_hot, levels.astype(jnp.float32), precision=lax.Precision.HIGHEST) / 1000.0
    )
    bus_ids = jnp.arange(bus_count, dtype=jnp.int32)
    area_sens = sensitivity[0]
    groups = lax.axis_size("feeder")
    block_area = area_ids.reshape(groups, per_dev)
    member_ids = jnp.arange(per_dev, dtype=jnp.int32)
    same_area = block_area[:, :, None] == block_area[:, None, :]
    earlier = member_ids[None, :] < member_ids[:, None]
    slot_ids = jnp.sum((same_area & earlier[None, :, :]).astype(jnp.int32), axis=2)
    my_area = lax.dynamic_index_in_dim(block_area, owner, 0, keepdims=False)
    my_slot = lax.dynamic_index_in_dim(slot_ids, owner, 0, keepdims=False)
    group_ids = jnp.arange(groups, dtype=jnp.int32)
    slot_range = jnp.arange(CAP, dtype=jnp.int32)
    outgoing = (
        (my_area[:, None, None] == group_ids[None, :, None])
        & (my_slot[:, None, None] == slot_range[None, None, :])
    ).astype(jnp.float32)
    send_flow = jnp.einsum("fdc,fkr->dckr", outgoing, head_flow, precision=lax.Precision.HIGHEST)
    recv_flow = lax.all_to_all(send_flow, "feeder", split_axis=0, concat_axis=0, tiled=True)
    match = (
        (block_area[:, None, :] == owner) & (slot_ids[:, None, :] == slot_range[None, :, None])
    ).astype(jnp.float32)
    block_bus = (head_bus.reshape(groups, per_dev)[:, :, None] == bus_ids[None, None, :]).astype(
        jnp.float32
    )
    slot_bus = jnp.einsum("sca,sab->scb", match, block_bus, precision=lax.Precision.HIGHEST)
    bus_flow = jnp.einsum("scb,sckr->kbr", slot_bus, recv_flow, precision=lax.Precision.HIGHEST)
    volt_shift = jnp.einsum("kbe,ker->br", area_sens, bus_flow, precision=lax.Precision.HIGHEST)
    volts = jnp.einsum("scb,br->scr", slot_bus, volt_shift, precision=lax.Precision.HIGHEST)
    knot_count = knot_volts.shape[1]
    filled = jnp.sum(match, axis=2)
    slot_volts = jnp.einsum(
        "sca,sak->sck",
        match,
        knot_volts.reshape(groups, per_dev, knot_count),
        precision=lax.Precision.HIGHEST,
    )
    slot_volts = (
        slot_volts
        + (1.0 - filled)[:, :, None] * jnp.arange(knot_count, dtype=jnp.float32)[None, None, :]
    )
    slot_levels = jnp.einsum(
        "sca,sak->sck",
        match,
        knot_levels.reshape(groups, per_dev, knot_count),
        precision=lax.Precision.HIGHEST,
    )
    settings = setpoint_rule(volts, slot_volts, slot_levels)
    returned = lax.all_to_all(settings, "feeder", split_axis=0, concat_axis=0, tiled=True)
    mine_back = jnp.einsum("fdc,dcr->fr", outgoing, returned, precision=lax.Precision.HIGHEST)
    return mine_back.reshape(per_dev, span_len, scenarios)


def solution(mesh):
    return jax.shard_map(
        per_device,
        mesh=mesh,
        in_specs=(
            P("feeder", None, "tm", None),
            P("feeder", None, None),
            P("feeder", "tm", None),
            P("feeder"),
            P("feeder", None, None),
            P(),
            P(),
            P(),
            P(),
            P(),
            P("feeder", None, None, None),
        ),
        out_specs=P("feeder", "tm", None),
        check_vma=False,
    )
```

profile of v0, /device:TPU:4, one launch (start us, length us, event | category | flops | bytes accessed | tf_op | source)
XLA Modules:
  0.0 145.7 jit_solution(7219737192449498526)
XLA Ops:
  0.0 0.8 constant_dynamic-update-slice_fusion.7
  0.8 0.8 fusion.36
  1.6 0.7 constant_dynamic-update-slice_fusion.6
  2.4 0.8 constant_dynamic-update-slice_fusion.5
  3.1 0.8 constant_dynamic-update-slice_fusion.4
  3.9 0.7 constant_dynamic-update-slice_fusion.3
  4.6 0.8 constant_dynamic-update-slice_fusion.2
  5.4 0.7 fusion.37
  6.1 5.8 %broadcast_multiply_fusion = f32[16,64,6,256]{3,1,2,0:T(8,128)S(1)} fusion(f32[16,256]{1,0:T(8,128)S(1)} %fusion.37, bf16[16,64,6,512]{3,1,2,0:T(8,128)(2,1)} %param.13, bf16[16,512,256]{2,1,0:T(8,128)(2,1)} %param.14), kind=kOutput, calls=%fused_computation.6 | convolution fusion | flops 1612185600 | bytes 16793600 | tf_op jit(solution)/shard_map/fctn,fns->fcts/dot_general | solution.py:47
  11.9 1.1 fusion.16
  13.0 1.2 constant_dynamic-update-slice_fusion.1
  14.2 1.1 fusion.19
  15.3 1.3 constant_dynamic-update-slice_fusion
  16.6 0.8 fusion.10
  17.5 1.1 fusion.20
  18.6 1.3 fusion.15
  19.9 0.1 broadcast.96
  20.0 84.6 %while.10 = (s32[]{:T(128)}, f32[16,64,256]{2,1,0:T(8,128)S(1)}, f32[16,256]{1,0:T(8,128)S(1)}, f32[16,64,256]{2,1,0:T(8,128)S(1)}, s32[]{:T(128)}) while((s32[]{:T(128)}, f32[16,64,256]{2,1,0:T(8,128)S(1)}, f32[16,256]{1,0:T(8,128)S(1)}, f32[16,64,256]{2,1,0:T(8,128)S(1)}, s32[]{:T(128)}) %tuple.53), condition=%wide.region_3.4_spmd, body=%wide.region_2.0_spmd.sunk | while | flops 524290 | bytes 7356517 | solution.py:64
  20.0 1.2 multiply_add_fusion.7
  21.1 3.4 %collective-permute-start = (f32[16,64,256]{2,1,0:T(8,128)}, f32[16,64,256]{2,1,0:T(8,128)S(1)}, u32[]{:S(2)}, u32[]{:S(2)}) collective-permute-start(f32[16,64,256]{2,1,0:T(8,128)} %multiply_add_fusion.7), channel_id=1, source_target_pairs={{0,1},{1,2},{2,3},{4,5},{5,6},{6,7},{8,9},{9,10},{10,11},{12,13},{... | collective-permute-start | bytes 3145736 | tf_op jit(solution)/shard_map/while/body/eval_jaxpr/ppermute | solution.py:12
  24.5 24.5 %collective-permute-done = f32[16,64,256]{2,1,0:T(8,128)S(1)} collective-permute-done((f32[16,64,256]{2,1,0:T(8,128)}, f32[16,64,256]{2,1,0:T(8,128)S(1)}, u32[]{:S(2)}, u32[]{:S(2)}) %collective-permute-start) | collective-permute-done | bytes 1048608 | tf_op jit(solution)/shard_map/while/body/eval_jaxpr/ppermute | solution.py:12
  49.0 1.2 multiply_add_fusion.7
  50.2 2.5 %collective-permute-start = (f32[16,64,256]{2,1,0:T(8,128)}, f32[16,64,256]{2,1,0:T(8,128)S(1)}, u32[]{:S(2)}, u32[]{:S(2)}) collective-permute-start(f32[16,64,256]{2,1,0:T(8,128)} %multiply_add_fusion.7), channel_id=1, source_target_pairs={{0,1},{1,2},{2,3},{4,5},{5,6},{6,7},{8,9},{9,10},{10,11},{12,13},{... | collective-permute-start | bytes 3145736 | tf_op jit(solution)/shard_map/while/body/eval_jaxpr/ppermute | solution.py:12
  52.7 24.5 %collective-permute-done = f32[16,64,256]{2,1,0:T(8,128)S(1)} collective-permute-done((f32[16,64,256]{2,1,0:T(8,128)}, f32[16,64,256]{2,1,0:T(8,128)S(1)}, u32[]{:S(2)}, u32[]{:S(2)}) %collective-permute-start) | collective-permute-done | bytes 1048608 | tf_op jit(solution)/shard_map/while/body/eval_jaxpr/ppermute | solution.py:12
  77.2 1.2 multiply_add_fusion.7
  78.4 1.9 %collective-permute-start = (f32[16,64,256]{2,1,0:T(8,128)}, f32[16,64,256]{2,1,0:T(8,128)S(1)}, u32[]{:S(2)}, u32[]{:S(2)}) collective-permute-start(f32[16,64,256]{2,1,0:T(8,128)} %multiply_add_fusion.7), channel_id=1, source_target_pairs={{0,1},{1,2},{2,3},{4,5},{5,6},{6,7},{8,9},{9,10},{10,11},{12,13},{... | collective-permute-start | bytes 3145736 | tf_op jit(solution)/shard_map/while/body/eval_jaxpr/ppermute | solution.py:12
  80.3 24.3 %collective-permute-done = f32[16,64,256]{2,1,0:T(8,128)S(1)} collective-permute-done((f32[16,64,256]{2,1,0:T(8,128)}, f32[16,64,256]{2,1,0:T(8,128)S(1)}, u32[]{:S(2)}, u32[]{:S(2)}) %collective-permute-start) | collective-permute-done | bytes 1048608 | tf_op jit(solution)/shard_map/while/body/eval_jaxpr/ppermute | solution.py:12
  104.6 16.8 %fusion.6 = f32[16,2,6,64]{3,1,2,0:T(2,128)S(1)} fusion(f32[16,2,256]{2,1,0:T(2,128)S(1)} %copy-done.1, f32[16,64,6,256]{3,1,0,2:T(8,128)} %fusion.15, f32[16,64,256]{2,1,0:T(8,128)S(1)} %get-tuple-element.27, f32[16,6,256]{2,0,1:T(8,128)S(1)} %get-tuple-element.42), kind=kOutput, calls=%fused_computation.8 | convolution fusion | flops 40894464 | bytes 7520256 | tf_op jit(solution)/shard_map/fcts,fks->fktc/dot_general | solution.py:69
  121.4 0.1 reshape.121
  121.5 0.5 broadcast.104
  122.0 0.7 reduce.3
  122.6 0.1 reshape_squeeze.3
  122.7 0.3 convert_reduce_fusion
  123.1 0.1 fusion.41
  123.2 0.7 copy.235
  123.9 4.9 %all-to-all-start = ((f32[8,2,2,384]{3,2,1,0:T(2,128)}), f32[8,2,2,384]{3,2,1,0:T(2,128)S(1)}, u32[]{:S(2)}, u32[]{:S(2)}) async-start(f32[8,2,2,384]{3,2,1,0:T(2,128)} %copy.235), calls=%async_computation | async-start | bytes 98304 | tf_op jit(solution)/shard_map/all_to_all | solution.py:100
  128.8 0.1 eq.124
  128.8 0.1 convert_reduce_fusion.1
  128.9 0.2 fusion.21
  129.2 0.2 convolution_multiply_fusion
  129.4 0.1 reshape.115
  129.4 0.2 fusion.25
  129.7 0.1 copy.226
  129.8 0.1 copy.225
  129.8 0.2 convolution_multiply_fusion.1
  130.0 0.1 reshape.114
  130.1 0.2 fusion.27
  130.3 0.1 fusion.62
  130.5 0.1 copy.252
  130.6 0.1 copy.263
  130.7 0.1 copy.253
  130.7 0.1 copy.259
  130.8 0.1 copy.260
  130.9 0.1 copy.261
  131.0 0.1 copy.262
  131.1 0.1 copy.264
  131.3 3.3 %all-to-all-done = f32[8,2,2,384]{3,2,1,0:T(2,128)S(1)} async-done(((f32[8,2,2,384]{3,2,1,0:T(2,128)}), f32[8,2,2,384]{3,2,1,0:T(2,128)S(1)}, u32[]{:S(2)}, u32[]{:S(2)}) %all-to-all-start) | async-done | bytes 49184 | tf_op jit(solution)/shard_map/all_to_all | solution.py:100
  134.6 0.8 convolution_bitcast_fusion
  135.4 0.8 fusion.17
  136.2 0.5 multiply_add_fusion.2
  136.8 8.1 %all_to_all.10 = f32[8,2,384]{2,1,0:T(2,128)S(1)} all-to-all(f32[8,2,384]{2,1,0:T(2,128)S(1)} %copy.245), channel_id=1, replica_groups=mesh['feeder'=8,'tm'=4] {'feeder'}, dimensions={0} | all-to-all | bytes 49152 | tf_op jit(solution)/shard_map/all_to_all | solution.py:130
  144.8 0.2 convolution_bitcast_fusion.1
  145.0 0.1 reshape.117
  145.1 0.6 copy.247
  (26 shorter events, 0.1 us)
Async XLA Ops:
  0.0 135.4 %copy-start = (f32[1,2,256,256]{3,2,1,0:T(8,128)S(1)}, f32[1,2,256,256]{3,2,1,0:T(8,128)}, u32[]{:S(2)}) copy-start(f32[1,2,256,256]{3,2,1,0:T(8,128)} %param.23) | copy-start | bytes 1572868
  20.0 84.6 %copy-start.1 = (f32[16,2,256]{2,1,0:T(2,128)S(1)}, f32[16,2,256]{2,1,0:T(2,128)}, u32[]{:S(2)}) copy-start(f32[16,2,256]{2,1,0:T(2,128)} %param.17) | copy-start | bytes 98308
  21.1 27.9 %collective-permute-start = (f32[16,64,256]{2,1,0:T(8,128)}, f32[16,64,256]{2,1,0:T(8,128)S(1)}, u32[]{:S(2)}, u32[]{:S(2)}) collective-permute-start(f32[16,64,256]{2,1,0:T(8,128)} %multiply_add_fusion.7), channel_id=1, source_target_pairs={{0,1},{1,2},{2,3},{4,5},{5,6},{6,7},{8,9},{9,10},{10,11},{12,13},{... | collective-permute-start | bytes 3145736 | tf_op jit(solution)/shard_map/while/body/eval_jaxpr/ppermute | solution.py:12
  50.2 27.0 %collective-permute-start = (f32[16,64,256]{2,1,0:T(8,128)}, f32[16,64,256]{2,1,0:T(8,128)S(1)}, u32[]{:S(2)}, u32[]{:S(2)}) collective-permute-start(f32[16,64,256]{2,1,0:T(8,128)} %multiply_add_fusion.7), channel_id=1, source_target_pairs={{0,1},{1,2},{2,3},{4,5},{5,6},{6,7},{8,9},{9,10},{10,11},{12,13},{... | collective-permute-start | bytes 3145736 | tf_op jit(solution)/shard_map/while/body/eval_jaxpr/ppermute | solution.py:12
  78.4 26.2 %collective-permute-start = (f32[16,64,256]{2,1,0:T(8,128)}, f32[16,64,256]{2,1,0:T(8,128)S(1)}, u32[]{:S(2)}, u32[]{:S(2)}) collective-permute-start(f32[16,64,256]{2,1,0:T(8,128)} %multiply_add_fusion.7), channel_id=1, source_target_pairs={{0,1},{1,2},{2,3},{4,5},{5,6},{6,7},{8,9},{9,10},{10,11},{12,13},{... | collective-permute-start | bytes 3145736 | tf_op jit(solution)/shard_map/while/body/eval_jaxpr/ppermute | solution.py:12
  104.6 17.4 %copy-start.5 = (s32[128,1]{0,1:T(1,128)S(1)}, s32[128,1]{0,1:T(1,128)}, u32[]{:S(2)}) copy-start(s32[128,1]{0,1:T(1,128)} %param.18) | copy-start | bytes 1540
  104.6 24.2 %copy-start.2 = (s32[128]{0:T(128)S(1)}, s32[128]{0:T(128)}, u32[]{:S(2)}) copy-start(s32[128]{0:T(128)} %param.19) | copy-start | bytes 1540
  104.6 24.6 %copy-start.3 = (s32[16,8]{0,1:T(8,128)S(1)}, s32[16,8]{0,1:T(8,128)}, u32[]{:S(2)}) copy-start(s32[16,8]{0,1:T(8,128)} %param.21) | copy-start | bytes 1540
  104.6 24.6 %copy-start.6 = (s32[128]{0:T(128)S(1)}, s32[128]{0:T(128)}, u32[]{:S(2)}) copy-start(s32[128]{0:T(128)} %param.20) | copy-start | bytes 1540
  104.6 25.3 %copy-start.4 = (s32[16,8]{0,1:T(8,128)S(1)}, s32[16,8]{0,1:T(8,128)}, u32[]{:S(2)}) copy-start(s32[16,8]{0,1:T(8,128)} %param.22) | copy-start | bytes 1540
  123.9 10.7 %all-to-all-start = ((f32[8,2,2,384]{3,2,1,0:T(2,128)}), f32[8,2,2,384]{3,2,1,0:T(2,128)S(1)}, u32[]{:S(2)}, u32[]{:S(2)}) async-start(f32[8,2,2,384]{3,2,1,0:T(2,128)} %copy.235), calls=%async_computation | async-start | bytes 98304 | tf_op jit(solution)/shard_map/all_to_all | solution.py:100
where the time goes:
time: 147 us; the launch traced here: 146 us
  waiting for transfers between devices  76.6 us (52%)
  matrix products  26.1 us (18%)
  other arithmetic  17.8 us (12%)
  starting transfers between devices  12.7 us (9%)
  blocking collectives  8.06 us (5%)
  local copies, waits for them, and re-layouts  4.22 us (3%)
    ppermute x3, waiting for transfers between devices, passed_along(): return lax.ppermute(block, axis, route)  73.3 us
    dot_general x1, matrix products, per_device(): jnp.einsum('fcts,fks->fktc', states, out_map, precision=lax.Precision.HIG...  16.8 us
    unnamed x10, other arithmetic  9.44 us
    all_to_all x1, blocking collectives, per_device(): lax.all_to_all(settings, 'feeder', split_axis=0, concat_axis=0, tiled=True)  8.06 us
    ppermute x3, starting transfers between devices, passed_along(): return lax.ppermute(block, axis, route)  7.78 us
    dot_general x1, matrix products, per_device(): jnp.einsum('fctn,fns->fcts', node_load, drive_map, preferred_element_type...  5.8 us
    all_to_all x1, starting transfers between devices, per_device(): lax.all_to_all(send_flow, 'feeder', split_axis=0, concat_axis=0, tiled=True)  4.88 us
    add x3, other arithmetic, one_turn(): local_state + decay_prod[:, None, :] * incoming  3.47 us
  transfers between devices with their start and end apart: 4, of which 4 were waited for; matrix products, arithmetic and copies ran while one was open for 2% of the time, Pallas kernels for 0%

commit v1 on v0

v1 whole, which is shorter than its diff:
```python
import functools

import jax
import jax.numpy as jnp
from jax import lax
from jax.experimental import pallas as pl
from jax.experimental.pallas import tpu as pltpu
from jax.sharding import PartitionSpec as P

HIGH = lax.Precision.HIGHEST
NT = (((1,), (1,)), ((), ()))
MESH = pl.DeviceIdType.MESH


def split(value):
    upper = value.astype(jnp.bfloat16).astype(jnp.float32)
    return upper, value - upper


def kernel(
    groups,
    turns,
    load_hbm,
    map_hbm,
    decay_ref,
    counts_ref,
    out_map_ref,
    area_ref,
    bus_ref,
    rule_ref,
    knots_ref,
    levels_ref,
    sens_hbm,
    out_ref,
    load_ref,
    map_ref,
    sens_ref,
    later_decay,
    pair_send,
    pair_recv,
    weight_ref,
    rule_vals,
    flow_ref,
    flow_send,
    flow_recv,
    volt_send,
    volt_recv,
    load_sem,
    map_sem,
    sens_sem,
    decay_sems,
    pair_sems,
    flow_sems,
    volt_sems,
):
    group, turn = lax.axis_index("feeder"), lax.axis_index("tm")
    per_dev, span, scen, nodes = load_ref.shape
    width = map_ref.shape[2]
    half = per_dev // 2
    couples = span // 2
    feeders = bus_ref.shape[1]
    buses = sens_ref.shape[1]
    rows = weight_ref.shape[1] // per_dev
    later_rows = (rows - 8) // 2
    piece = couples * 2 * half

    sens_copy = pltpu.make_async_copy(sens_hbm.at[0], sens_ref, sens_sem)
    sens_copy.start()

    def load_copies(f):
        return (
            pltpu.make_async_copy(load_hbm.at[f], load_ref.at[f], load_sem.at[f]),
            pltpu.make_async_copy(map_hbm.at[f], map_ref.at[f], map_sem.at[f]),
        )

    def start_loads(f, carry):
        for copy in load_copies(f):
            copy.start()
        return carry

    lax.fori_loop(0, per_dev, start_loads, 0)

    barrier = pltpu.get_barrier_semaphore()
    for step in range(1, turns):
        pl.semaphore_signal(
            barrier,
            inc=1,
            device_id=(group, lax.rem(turn + step, turns)),
            device_id_type=MESH,
        )
    for step in range(1, groups):
        pl.semaphore_signal(
            barrier,
            inc=1,
            device_id=(lax.rem(group + step, groups), turn),
            device_id_type=MESH,
        )
    pl.semaphore_wait(barrier, turns + groups - 2)

    def decay_copy(step):
        return pltpu.make_async_remote_copy(
            src_ref=decay_ref,
            dst_ref=later_decay.at[step - 1],
            send_sem=decay_sems.at[0, step - 1],
            recv_sem=decay_sems.at[1, step - 1],
            device_id=(group, turn - step),
            device_id_type=MESH,
        )

    for step in range(1, turns):

        @pl.when(turn >= step)
        def _():
            decay_copy(step).start()

    bus_ids = lax.broadcasted_iota(jnp.int32, (buses, feeders), 0)
    owned = (bus_ids == bus_ref[...]) & (area_ref[...] == group)
    hot = jnp.where(owned, 1.0, 0.0)
    hot_rows = hot.T
    sens_copy.wait()
    for k in range(2):
        picked = lax.dot_general(
            hot_rows, sens_ref[k], NT, precision=HIGH, preferred_element_type=jnp.float32
        )
        pairs = jnp.dot(picked, hot, precision=HIGH, preferred_element_type=jnp.float32)
        pair_send[:, k] = pairs.reshape(groups, per_dev, feeders)

    def pair_copy(step):
        target = lax.rem(group + step, groups)
        return pltpu.make_async_remote_copy(
            src_ref=pair_send.at[target],
            dst_ref=pair_recv.at[step - 1],
            send_sem=pair_sems.at[0, step - 1],
            recv_sem=pair_sems.at[1, step - 1],
            device_id=(target, turn),
            device_id_type=MESH,
        )

    for step in range(1, groups):
        pair_copy(step).start()

    rules = knots_ref.shape[1]
    rule_ids = lax.broadcasted_iota(jnp.int32, (rules, feeders), 0)
    rule_hot = jnp.where(rule_ids == rule_ref[...], 1.0, 0.0)
    table = jnp.concatenate(
        [knots_ref[...].astype(jnp.float32), levels_ref[...].astype(jnp.float32)], axis=0
    )
    chosen = jnp.dot(table, rule_hot, precision=HIGH, preferred_element_type=jnp.float32)
    rule_vals[...] = (chosen / 1000.0).T

    member = lax.broadcasted_iota(jnp.int32, (per_dev, width), 0)
    state_ids = lax.broadcasted_iota(jnp.int32, (per_dev, width), 1)
    limit = jnp.zeros((per_dev, width), jnp.int32)
    for f in range(per_dev):
        limit = jnp.where(member == f, counts_ref[f], limit)
    maps = [jnp.where(state_ids < limit, out_map_ref[:, k, :], 0.0) for k in range(2)]

    def put_rows(row, value):
        for lane in range(width // 128):
            weight_ref[lane, pl.ds(row, per_dev, stride=rows), :] = value[
                :, lane * 128 : (lane + 1) * 128
            ]

    for k in range(2):
        put_rows(k, maps[k])
    for step in range(1, turns):

        @pl.when(turn >= step)
        def _():
            decay_copy(step).wait_send()

        @pl.when(turn + step < turns)
        def _():
            decay_copy(step).wait_recv()

    product = jnp.ones((per_dev, width), jnp.float32)
    for step in range(turns - 1):
        for t in range(span):
            product = product * later_decay[step, t]
            for k in range(2):
                row = 8 + (t % 2) * later_rows + (step * couples + t // 2) * 2 + k
                put_rows(row, maps[k] * product)

    def feeder_flow(part, index, carry):
        f = part * half + index
        for copy in load_copies(f):
            copy.wait()
        drive = jnp.dot(
            load_ref[f].reshape(span * scen, nodes),
            map_ref[f],
            preferred_element_type=jnp.float32,
        )
        states = [drive[:scen]]
        for t in range(1, span):
            retain = decay_ref[t, pl.ds(f, 1), :]
            states.append(retain * states[-1] + drive[t * scen : (t + 1) * scen])
        upper, lower = split(jnp.concatenate(states, axis=0))
        both = jnp.concatenate([upper.astype(jnp.bfloat16), lower.astype(jnp.bfloat16)], axis=1)
        first = pl.multiple_of(f * rows, 8)
        weight = jnp.concatenate(
            [weight_ref[lane, pl.ds(first, rows), :] for lane in range(width // 128)], axis=1
        )
        w_upper, w_lower = split(weight)

        def doubled(start, stop):
            stacked = jnp.concatenate([w_upper[start:stop], w_lower[start:stop]], axis=0)
            stacked = stacked.astype(jnp.bfloat16)
            return jnp.concatenate([stacked, stacked], axis=1)

        local = lax.dot_general(doubled(0, 8), both, NT, preferred_element_type=jnp.float32)
        local = local[:8] + local[8:]
        for couple in range(couples):
            flow_ref[part, pl.ds(couple * 2 * half + index, 2, stride=half), :] = local[
                :2, couple * 2 * scen : (couple + 1) * 2 * scen
            ]
        if turns > 1:
            later = lax.dot_general(
                doubled(8, rows), both[(span - 1) * scen :], NT, preferred_element_type=jnp.float32
            )
            later = later[: 2 * later_rows] + later[2 * later_rows :]
            flow_send[part, pl.ds(index, later_rows, stride=half), :] = jnp.concatenate(
                [later[:later_rows], later[later_rows:]], axis=1
            )
        return carry

    def flow_copy(part, step):
        return pltpu.make_async_remote_copy(
            src_ref=flow_send.at[part, pl.ds((step - 1) * piece, piece)],
            dst_ref=flow_recv.at[part, step - 1],
            send_sem=flow_sems.at[0, part, step - 1],
            recv_sem=flow_sems.at[1, part, step - 1],
            device_id=(group, turn + step),
            device_id_type=MESH,
        )

    for part in range(2):
        lax.fori_loop(0, half, functools.partial(feeder_flow, part), 0)
        for step in range(1, turns):

            @pl.when(turn + step < turns)
            def _():
                flow_copy(part, step).start()

    effect = pair_send[group]
    for step in range(1, groups):
        pair_copy(step).wait()
        effect = effect + pair_recv[step - 1]
    effect = jnp.concatenate(
        [effect[k, part * half : (part + 1) * half] for part in range(2) for k in range(2)], axis=0
    ).T

    for part in range(2):
        for step in range(1, turns):

            @pl.when(turn >= step)
            def _():
                flow_copy(part, step).wait_recv()
                flow_ref[part] = flow_ref[part] + flow_recv[part, step - 1]

    for couple in range(couples):
        sources = jnp.concatenate(
            [flow_ref[part, couple * 2 * half : (couple + 1) * 2 * half] for part in range(2)],
            axis=0,
        )
        shift = jnp.dot(effect, sources, precision=HIGH, preferred_element_type=jnp.float32)
        volt_send[:, couple] = shift.reshape(groups, per_dev, 2 * scen)

    def volt_copy(step):
        target = lax.rem(group + step, groups)
        return pltpu.make_async_remote_copy(
            src_ref=volt_send.at[target],
            dst_ref=volt_recv.at[step - 1],
            send_sem=volt_sems.at[0, step - 1],
            recv_sem=volt_sems.at[1, step - 1],
            device_id=(target, turn),
            device_id_type=MESH,
        )

    for step in range(1, groups):
        volt_copy(step).start()

    mine = rule_vals[pl.ds(pl.multiple_of(group * per_dev, 8), per_dev), :]
    knot_count = knots_ref.shape[0]
    knots = [mine[:, i : i + 1] for i in range(knot_count)]
    levels = [mine[:, knot_count + i : knot_count + i + 1] for i in range(knot_count)]
    spans = [knots[i + 1] - knots[i] for i in range(knot_count - 1)]
    slopes = [(levels[i + 1] - levels[i]) / spans[i] for i in range(knot_count - 1)]
    volts = volt_send[group]
    for step in range(1, groups):
        volt_copy(step).wait_recv()
        volts = volts + volt_recv[step - 1]
    for couple in range(couples):
        value = volts[couple]
        result = levels[0] + jnp.zeros_like(value)
        for i in range(knot_count - 1):
            inside = jnp.minimum(jnp.maximum(value - knots[i], 0.0), spans[i])
            result = result + slopes[i] * inside
        out_ref[2 * couple] = result[:, :scen]
        out_ref[2 * couple + 1] = result[:, scen:]

    for step in range(1, groups):
        volt_copy(step).wait_send()
    for part in range(2):
        for step in range(1, turns):

            @pl.when(turn + step < turns)
            def _():
                flow_copy(part, step).wait_send()


def per_device(
    node_load,
    drive_map,
    decay_rate,
    counts,
    out_map,
    area_of,
    head_bus,
    rule_of,
    rule_knots,
    levels,
    sensitivity,
):
    groups, turns = lax.axis_size("feeder"), lax.axis_size("tm")
    per_dev, scen, span, nodes = node_load.shape
    width = drive_map.shape[2]
    feeders = head_bus.shape[0]
    buses = sensitivity.shape[2]
    half, couples = per_dev // 2, span // 2
    later_rows = -(-(turns - 1) * span // 8) * 8
    rows = 8 + 2 * later_rows
    piece = couples * 2 * half
    vmem = pl.BlockSpec(memory_space=pltpu.VMEM)
    hbm = pl.BlockSpec(memory_space=pltpu.HBM)
    smem = pl.BlockSpec(memory_space=pltpu.SMEM)
    f32 = jnp.float32
    dma = pltpu.SemaphoreType.DMA
    settings = pl.pallas_call(
        functools.partial(kernel, groups, turns),
        out_shape=jax.ShapeDtypeStruct((span, per_dev, scen), f32),
        in_specs=[hbm, hbm, vmem, smem, vmem, vmem, vmem, vmem, vmem, vmem, hbm],
        out_specs=vmem,
        scratch_shapes=[
            pltpu.VMEM((per_dev, span, scen, nodes), node_load.dtype),
            pltpu.VMEM((per_dev, nodes, width), drive_map.dtype),
            pltpu.VMEM((2, buses, buses), f32),
            pltpu.VMEM((turns - 1, span, per_dev, width), f32),
            pltpu.VMEM((groups, 2, per_dev, feeders), f32),
            pltpu.VMEM((groups - 1, 2, per_dev, feeders), f32),
            pltpu.VMEM((width // 128, per_dev * rows, 128), f32),
            pltpu.VMEM((feeders, 2 * rule_knots.shape[1]), f32),
            pltpu.VMEM((2, piece, 2 * scen), f32),
            pltpu.VMEM((2, later_rows * half, 2 * scen), f32),
            pltpu.VMEM((2, turns - 1, piece, 2 * scen), f32),
            pltpu.VMEM((groups, couples, per_dev, 2 * scen), f32),
            pltpu.VMEM((groups - 1, couples, per_dev, 2 * scen), f32),
            dma((per_dev,)),
            dma((per_dev,)),
            dma,
            dma((2, turns - 1)),
            dma((2, groups - 1)),
            dma((2, 2, turns - 1)),
            dma((2, groups - 1)),
        ],
        compiler_params=pltpu.CompilerParams(collective_id=0, has_side_effects=True),
    )(
        jnp.transpose(node_load, (0, 2, 1, 3)),
        drive_map,
        jnp.transpose(decay_rate, (1, 0, 2)),
        counts,
        out_map,
        area_of.reshape(1, feeders),
        head_bus.reshape(1, feeders),
        rule_of.reshape(1, feeders),
        rule_knots.T,
        levels.T,
        sensitivity,
    )
    return jnp.transpose(settings, (1, 0, 2))


def solution(mesh):
    return jax.shard_map(
        per_device,
        mesh=mesh,
        in_specs=(
            P("feeder", None, "tm", None),
            P("feeder", None, None),
            P("feeder", "tm", None),
            P("feeder"),
            P("feeder", None, None),
            P(),
            P(),
            P(),
            P(),
            P(),
            P("feeder", None, None, None),
        ),
        out_specs=P("feeder", "tm", None),
        check_vma=False,
    )
```

time: 147 us -> 31.2 us (0.21)
  the two profiles are of different devices: /device:TPU:4 before, /device:TPU:29 now
where the time goes in v1:
time: 31.2 us; the launch traced here: 31 us
  Pallas kernels  29.6 us (95%)
  local copies, waits for them, and re-layouts  1.42 us (5%)
    pallas_call x1, Pallas kernels, per_device(): pl.pallas_call(functools.partial(kernel, groups, turns), out_shape=jax.Sh...  29.6 us
    unnamed x1, local copies, waits for them, and re-layouts  1.42 us

profile of v1, /device:TPU:29, one launch (start us, length us, event | category | flops | bytes accessed | tf_op | source)
XLA Modules:
  0.0 31.0 jit_solution(9539307261512885522)
XLA Ops:
  0.0 29.6 %shard_map.109 = f32[6,16,64]{2,1,0:T(8,128)} custom-call(bf16[16,6,64,512]{3,2,1,0:T(8,128)(2,1)} %bitcast.8, bf16[16,512,256]{2,1,0:T(8,128)(2,1)} %map_hbm.1, f32[6,16,256]{2,1,0:T(8,128)} %bitcast.10, s32[16]{0:T(128)} %counts_ref.1, f32[16,2,256]{2,1,0:T(2,128)} %out_map_ref.1, s32[1,128]{1,0:T(1,128)} %bitcast.13, s32[1,128]{1,0:T(1,128)} %bitcast.14, ...), custom_call_target="tpu_custom_call" | custom-call | tf_op jit(solution)/shard_map/pallas_call | solution.py:338
  29.6 1.4 %copy.13 = f32[16,6,64]{2,0,1:T(8,128)} copy(f32[16,6,64]{2,0,1:T(8,128)} %bitcast.9) | data formatting | bytes 49152

commit v2 on v1

--- a/solution.py
+++ b/solution.py
@@ -10,6 +10,7 @@
 HIGH = lax.Precision.HIGHEST
 NT = (((1,), (1,)), ((), ()))
 MESH = pl.DeviceIdType.MESH
+UNROLL = 4
 
 
 def split(value):
@@ -39,6 +40,8 @@
     pair_send,
     pair_recv,
     weight_ref,
+    state_ref,
+    column_ref,
     rule_vals,
     flow_ref,
     flow_send,
@@ -61,7 +64,7 @@
     feeders = bus_ref.shape[1]
     buses = sens_ref.shape[1]
     rows = weight_ref.shape[1] // per_dev
-    later_rows = (rows - 8) // 2
+    later_rows = rows // 2
     piece = couples * 2 * half
 
     sens_copy = pltpu.make_async_copy(sens_hbm.at[0], sens_ref, sens_sem)
@@ -95,7 +98,6 @@
             device_id=(lax.rem(group + step, groups), turn),
             device_id_type=MESH,
         )
-    pl.semaphore_wait(barrier, turns + groups - 2)
 
     def decay_copy(step):
         return pltpu.make_async_remote_copy(
@@ -106,12 +108,6 @@
             device_id=(group, turn - step),
             device_id_type=MESH,
         )
-
-    for step in range(1, turns):
-
-        @pl.when(turn >= step)
-        def _():
-            decay_copy(step).start()
 
     bus_ids = lax.broadcasted_iota(jnp.int32, (buses, feeders), 0)
     owned = (bus_ids == bus_ref[...]) & (area_ref[...] == group)
@@ -125,6 +121,14 @@
         pairs = jnp.dot(picked, hot, precision=HIGH, preferred_element_type=jnp.float32)
         pair_send[:, k] = pairs.reshape(groups, per_dev, feeders)
 
+    pl.semaphore_wait(barrier, turns + groups - 2)
+
+    for step in range(1, turns):
+
+        @pl.when(turn >= step)
+        def _():
+            decay_copy(step).start()
+
     def pair_copy(step):
         target = lax.rem(group + step, groups)
         return pltpu.make_async_remote_copy(
@@ -161,28 +165,17 @@
                 :, lane * 128 : (lane + 1) * 128
             ]
 
-    for k in range(2):
-        put_rows(k, maps[k])
-    for step in range(1, turns):
-
-        @pl.when(turn >= step)
-        def _():
-            decay_copy(step).wait_send()
-
-        @pl.when(turn + step < turns)
-        def _():
-            decay_copy(step).wait_recv()
-
-    product = jnp.ones((per_dev, width), jnp.float32)
-    for step in range(turns - 1):
-        for t in range(span):
-            product = product * later_decay[step, t]
-            for k in range(2):
-                row = 8 + (t % 2) * later_rows + (step * couples + t // 2) * 2 + k
-                put_rows(row, maps[k] * product)
-
-    def feeder_flow(part, index, carry):
-        f = part * half + index
+    parts = [split(m) for m in maps]
+    columns = [p[0] for p in parts] + [p[1] for p in parts]
+    blank = jnp.zeros((128 - 4 * per_dev, width), jnp.float32)
+    columns = jnp.concatenate(columns + [blank], axis=0).T.astype(jnp.bfloat16)
+    lane_ids = lax.rem(lax.broadcasted_iota(jnp.int32, (1, 128), 1), per_dev)
+    for f in range(per_dev):
+        own = columns * jnp.where(lane_ids == f, 1.0, 0.0).astype(jnp.bfloat16)
+        for copy in range(2):
+            first = (2 * f + copy) * width
+            column_ref[first : first + width] = own
+    def feeder_states(f, carry):
         for copy in load_copies(f):
             copy.wait()
         drive = jnp.dot(
@@ -195,32 +188,25 @@
             retain = decay_ref[t, pl.ds(f, 1), :]
             states.append(retain * states[-1] + drive[t * scen : (t + 1) * scen])
         upper, lower = split(jnp.concatenate(states, axis=0))
-        both = jnp.concatenate([upper.astype(jnp.bfloat16), lower.astype(jnp.bfloat16)], axis=1)
+        first = pl.multiple_of(2 * f * width, 128)
+        state_ref[:, pl.ds(first, width)] = upper.astype(jnp.bfloat16)
+        state_ref[:, pl.ds(first + width, width)] = lower.astype(jnp.bfloat16)
+        return carry
+
+    def later_flow(part, index, carry):
+        f = part * half + index
         first = pl.multiple_of(f * rows, 8)
         weight = jnp.concatenate(
             [weight_ref[lane, pl.ds(first, rows), :] for lane in range(width // 128)], axis=1
         )
-        w_upper, w_lower = split(weight)
-
-        def doubled(start, stop):
-            stacked = jnp.concatenate([w_upper[start:stop], w_lower[start:stop]], axis=0)
-            stacked = stacked.astype(jnp.bfloat16)
-            return jnp.concatenate([stacked, stacked], axis=1)
-
-        local = lax.dot_general(doubled(0, 8), both, NT, preferred_element_type=jnp.float32)
-        local = local[:8] + local[8:]
-        for couple in range(couples):
-            flow_ref[part, pl.ds(couple * 2 * half + index, 2, stride=half), :] = local[
-                :2, couple * 2 * scen : (couple + 1) * 2 * scen
-            ]
-        if turns > 1:
-            later = lax.dot_general(
-                doubled(8, rows), both[(span - 1) * scen :], NT, preferred_element_type=jnp.float32
-            )
-            later = later[: 2 * later_rows] + later[2 * later_rows :]
-            flow_send[part, pl.ds(index, later_rows, stride=half), :] = jnp.concatenate(
-                [later[:later_rows], later[later_rows:]], axis=1
-            )
+        stacked = jnp.concatenate(split(weight), axis=0).astype(jnp.bfloat16)
+        stacked = jnp.concatenate([stacked, stacked], axis=1)
+        end = state_ref[(span - 1) * scen :, pl.ds(pl.multiple_of(2 * f * width, 128), 2 * width)]
+        later = lax.dot_general(stacked, end, NT, preferred_element_type=jnp.float32)
+        later = later[:rows] + later[rows:]
+        flow_send[part, pl.ds(index, later_rows, stride=half), :] = jnp.concatenate(
+            [later[:later_rows], later[later_rows:]], axis=1
+        )
         return carry
 
     def flow_copy(part, step):
@@ -233,20 +219,44 @@
             device_id_type=MESH,
         )
 
+    lax.fori_loop(0, per_dev, feeder_states, 0, unroll=UNROLL)
+    for step in range(1, turns):
+
+        @pl.when(turn >= step)
+        def _():
+            decay_copy(step).wait_send()
+
+        @pl.when(turn + step < turns)
+        def _():
+            decay_copy(step).wait_recv()
+
+    product = jnp.ones((per_dev, width), jnp.float32)
+    for step in range(turns - 1):
+        for t in range(span):
+            product = product * later_decay[step, t]
+            for k in range(2):
+                row = (t % 2) * later_rows + (step * couples + t // 2) * 2 + k
+                put_rows(row, maps[k] * product)
+
     for part in range(2):
-        lax.fori_loop(0, half, functools.partial(feeder_flow, part), 0)
+        if turns > 1:
+            lax.fori_loop(0, half, functools.partial(later_flow, part), 0, unroll=UNROLL)
         for step in range(1, turns):
 
             @pl.when(turn + step < turns)
             def _():
                 flow_copy(part, step).start()
 
+    local = jnp.dot(state_ref[...], column_ref[...], preferred_element_type=jnp.float32).T
+    local = local[: 2 * per_dev] + local[2 * per_dev : 4 * per_dev]
+    flow_ref[...] = jnp.zeros_like(flow_ref)
+
     effect = pair_send[group]
     for step in range(1, groups):
         pair_copy(step).wait()
         effect = effect + pair_recv[step - 1]
     effect = jnp.concatenate(
-        [effect[k, part * half : (part + 1) * half] for part in range(2) for k in range(2)], axis=0
+        [effect[k, part * half : (part + 1) * half] for k in range(2) for part in range(2)], axis=0
     ).T
 
     for part in range(2):
@@ -258,10 +268,13 @@
                 flow_ref[part] = flow_ref[part] + flow_recv[part, step - 1]
 
     for couple in range(couples):
-        sources = jnp.concatenate(
-            [flow_ref[part, couple * 2 * half : (couple + 1) * 2 * half] for part in range(2)],
-            axis=0,
-        )
+        arrived = [
+            flow_ref[part, (couple * 2 + k) * half : (couple * 2 + k + 1) * half]
+            for k in range(2)
+            for part in range(2)
+        ]
+        sources = local[:, couple * 2 * scen : (couple + 1) * 2 * scen]
+        sources = sources + jnp.concatenate(arrived, axis=0)
         shift = jnp.dot(effect, sources, precision=HIGH, preferred_element_type=jnp.float32)
         volt_send[:, couple] = shift.reshape(groups, per_dev, 2 * scen)
 
@@ -328,7 +341,7 @@
     buses = sensitivity.shape[2]
     half, couples = per_dev // 2, span // 2
     later_rows = -(-(turns - 1) * span // 8) * 8
-    rows = 8 + 2 * later_rows
+    rows = max(2 * later_rows, 8)
     piece = couples * 2 * half
     vmem = pl.BlockSpec(memory_space=pltpu.VMEM)
     hbm = pl.BlockSpec(memory_space=pltpu.HBM)
@@ -348,6 +361,8 @@
             pltpu.VMEM((groups, 2, per_dev, feeders), f32),
             pltpu.VMEM((groups - 1, 2, per_dev, feeders), f32),
             pltpu.VMEM((width // 128, per_dev * rows, 128), f32),
+            pltpu.VMEM((span * scen, per_dev * 2 * width), jnp.bfloat16),
+            pltpu.VMEM((per_dev * 2 * width, 128), jnp.bfloat16),
             pltpu.VMEM((feeders, 2 * rule_knots.shape[1]), f32),
             pltpu.VMEM((2, piece, 2 * scen), f32),
             pltpu.VMEM((2, later_rows * half, 2 * scen), f32),

time: 31.2 us -> 25.4 us (0.81)
  the two profiles are of different devices: /device:TPU:29 before, /device:TPU:0 now
where the time goes in v2:
time: 25.4 us; the launch traced here: 25 us
  Pallas kernels  23.6 us (93%)
  local copies, waits for them, and re-layouts  1.42 us (6%)
    pallas_call x1, Pallas kernels, per_device(): pl.pallas_call(functools.partial(kernel, groups, turns), out_shape=jax.Sh...  23.6 us
    unnamed x1, local copies, waits for them, and re-layouts  1.42 us

profile of v2, /device:TPU:0, one launch (start us, length us, event | category | flops | bytes accessed | tf_op | source)
XLA Modules:
  0.0 25.0 jit_solution(17978210853044427247)
XLA Ops:
  0.0 23.6 %shard_map.109 = f32[6,16,64]{2,1,0:T(8,128)} custom-call(bf16[16,6,64,512]{3,2,1,0:T(8,128)(2,1)} %bitcast.8, bf16[16,512,256]{2,1,0:T(8,128)(2,1)} %map_hbm.1, f32[6,16,256]{2,1,0:T(8,128)} %bitcast.10, s32[16]{0:T(128)} %counts_ref.1, f32[16,2,256]{2,1,0:T(2,128)} %out_map_ref.1, s32[1,128]{1,0:T(1,128)} %bitcast.13, s32[1,128]{1,0:T(1,128)} %bitcast.14, ...), custom_call_target="tpu_custom_call" | custom-call | tf_op jit(solution)/shard_map/pallas_call | solution.py:351
  23.6 1.4 %copy.13 = f32[16,6,64]{2,0,1:T(8,128)} copy(f32[16,6,64]{2,0,1:T(8,128)} %bitcast.9) | data formatting | bytes 49152

commit v3 on v2

--- a/solution.py
+++ b/solution.py
@@ -10,7 +10,7 @@
 HIGH = lax.Precision.HIGHEST
 NT = (((1,), (1,)), ((), ()))
 MESH = pl.DeviceIdType.MESH
-UNROLL = 4
+UNROLL = 8
 
 
 def split(value):
@@ -112,13 +112,20 @@
     bus_ids = lax.broadcasted_iota(jnp.int32, (buses, feeders), 0)
     owned = (bus_ids == bus_ref[...]) & (area_ref[...] == group)
     hot = jnp.where(owned, 1.0, 0.0)
-    hot_rows = hot.T
+    hot_rows = hot.T.astype(jnp.bfloat16)
+    hot = hot.astype(jnp.bfloat16)
     sens_copy.wait()
     for k in range(2):
-        picked = lax.dot_general(
-            hot_rows, sens_ref[k], NT, precision=HIGH, preferred_element_type=jnp.float32
-        )
-        pairs = jnp.dot(picked, hot, precision=HIGH, preferred_element_type=jnp.float32)
+        picked = sum(
+            lax.dot_general(
+                hot_rows, term.astype(jnp.bfloat16), NT, preferred_element_type=jnp.float32
+            )
+            for term in split(sens_ref[k])
+        )
+        pairs = sum(
+            jnp.dot(term.astype(jnp.bfloat16), hot, preferred_element_type=jnp.float32)
+            for term in split(picked)
+        )
         pair_send[:, k] = pairs.reshape(groups, per_dev, feeders)
 
     pl.semaphore_wait(barrier, turns + groups - 2)
@@ -258,6 +265,8 @@
     effect = jnp.concatenate(
         [effect[k, part * half : (part + 1) * half] for k in range(2) for part in range(2)], axis=0
     ).T
+    upper, lower = split(effect)
+    effect = jnp.concatenate([upper, upper, lower], axis=1).astype(jnp.bfloat16)
 
     for part in range(2):
         for step in range(1, turns):
@@ -275,7 +284,9 @@
         ]
         sources = local[:, couple * 2 * scen : (couple + 1) * 2 * scen]
         sources = sources + jnp.concatenate(arrived, axis=0)
-        shift = jnp.dot(effect, sources, precision=HIGH, preferred_element_type=jnp.float32)
+        upper, lower = split(sources)
+        sources = jnp.concatenate([upper, lower, upper], axis=0).astype(jnp.bfloat16)
+        shift = jnp.dot(effect, sources, preferred_element_type=jnp.float32)
         volt_send[:, couple] = shift.reshape(groups, per_dev, 2 * scen)
 
     def volt_copy(step):

time: 25.4 us -> 24.8 us (0.976)
  Pallas kernels: 23.6 us -> 23.2 us
    pallas_call x1, Pallas kernels: 23.6 us -> 23.2 us  [per_device(): pl.pallas_call(functools.partial(kernel, groups, turns), out_shape=jax.Sh...]
where the time goes in v3:
time: 24.8 us; the launch traced here: 24.6 us
  Pallas kernels  23.2 us (94%)
  local copies, waits for them, and re-layouts  1.42 us (6%)
    pallas_call x1, Pallas kernels, per_device(): pl.pallas_call(functools.partial(kernel, groups, turns), out_shape=jax.Sh...  23.2 us
    unnamed x1, local copies, waits for them, and re-layouts  1.42 us

profile of v3, /device:TPU:0, one launch (start us, length us, event | category | flops | bytes accessed | tf_op | source)
XLA Modules:
  0.0 24.6 jit_solution(16141845004619465905)
XLA Ops:
  0.0 23.2 %shard_map.109 = f32[6,16,64]{2,1,0:T(8,128)} custom-call(bf16[16,6,64,512]{3,2,1,0:T(8,128)(2,1)} %bitcast.8, bf16[16,512,256]{2,1,0:T(8,128)(2,1)} %map_hbm.1, f32[6,16,256]{2,1,0:T(8,128)} %bitcast.10, s32[16]{0:T(128)} %counts_ref.1, f32[16,2,256]{2,1,0:T(2,128)} %out_map_ref.1, s32[1,128]{1,0:T(1,128)} %bitcast.13, s32[1,128]{1,0:T(1,128)} %bitcast.14, ...), custom_call_target="tpu_custom_call" | custom-call | tf_op jit(solution)/shard_map/pallas_call | solution.py:362
  23.2 1.4 %copy.13 = f32[16,6,64]{2,0,1:T(8,128)} copy(f32[16,6,64]{2,0,1:T(8,128)} %bitcast.9) | data formatting | bytes 49152

commit v4 on v3

--- a/solution.py
+++ b/solution.py
@@ -226,7 +226,7 @@
             device_id_type=MESH,
         )
 
-    lax.fori_loop(0, per_dev, feeder_states, 0, unroll=UNROLL)
+    lax.fori_loop(0, per_dev, feeder_states, 0, unroll=per_dev)
     for step in range(1, turns):
 
         @pl.when(turn >= step)

time: 24.8 us -> 26.1 us (1.052)
  Pallas kernels: 23.2 us -> 24.5 us
    pallas_call x1, Pallas kernels: 23.2 us -> 24.5 us  [per_device(): pl.pallas_call(functools.partial(kernel, groups, turns), out_shape=jax.Sh...]
where the time goes in v4:
time: 26.1 us; the launch traced here: 25.9 us
  Pallas kernels  24.5 us (94%)
  local copies, waits for them, and re-layouts  1.42 us (5%)
    pallas_call x1, Pallas kernels, per_device(): pl.pallas_call(functools.partial(kernel, groups, turns), out_shape=jax.Sh...  24.5 us
    unnamed x1, local copies, waits for them, and re-layouts  1.42 us

profile of v4, /device:TPU:0, one launch (start us, length us, event | category | flops | bytes accessed | tf_op | source)
XLA Modules:
  0.0 25.9 jit_solution(5917087838844443265)
XLA Ops:
  0.0 24.5 %shard_map.109 = f32[6,16,64]{2,1,0:T(8,128)} custom-call(bf16[16,6,64,512]{3,2,1,0:T(8,128)(2,1)} %bitcast.8, bf16[16,512,256]{2,1,0:T(8,128)(2,1)} %map_hbm.1, f32[6,16,256]{2,1,0:T(8,128)} %bitcast.10, s32[16]{0:T(128)} %counts_ref.1, f32[16,2,256]{2,1,0:T(2,128)} %out_map_ref.1, s32[1,128]{1,0:T(1,128)} %bitcast.13, s32[1,128]{1,0:T(1,128)} %bitcast.14, ...), custom_call_target="tpu_custom_call" | custom-call | tf_op jit(solution)/shard_map/pallas_call | solution.py:362
  24.5 1.4 %copy.13 = f32[16,6,64]{2,0,1:T(8,128)} copy(f32[16,6,64]{2,0,1:T(8,128)} %bitcast.9) | data formatting | bytes 49152
